TPU v7x, 32 devices: a whole 2x2x4 slice. The times are simulated.
32 devices in a mesh: grp: 2 (over y), pb: 4 (over z), re: 2 (over x), ka: 2 (over core).
Axes of the slice: x: 2, y: 2, z: 4, core: 2. Of those that a mesh axis runs over, the one named last changes fastest.
Arguments:
- g_wann: bfloat16 [2, 1024, 128, 256], P(None, 'pb', ('grp', 're'), 'ka'), parts along dimension 2, may hold values from -0.0234375 to 0.0234375
- phonon_phase: bfloat16 [2, 2048, 1024], P(None, 'pb'), may hold values from -1 to 1, as said below
- electron_phase: bfloat16 [2, 8, 64], replicated, may hold values from -1 to 1, as said below
Outputs:
- coupling: float32 [16, 2, 2048, 256], P(('grp', 're'), None, 'pb', 'ka'), parts along dimension 0
There are 2 independent parts, one for each index of `grp`. A program takes and returns all parts, laid end to end along the dimension named above; an argument that names none is the same for every part. Nothing has to cross between parts.
Inputs may be any that keep to these rules, and one draw needn't show every extreme that they name: `phonon_phase`: entries 0 and 1 along the first dimension are the cosine and sine of one angle. `electron_phase`: entries 0 and 1 along the first dimension are the cosine and sine of one angle.
All inputs are finite; a program needn't handle non-finite values.
Results may differ from a plain program's by a relative error of at most 0.0029.
Values may be sent and summed in bfloat16 or wider, within the bound.
A program may use at most 64 MiB of HBM per device.

v0:
```python
import jax
import jax.numpy as jnp
from jax import lax
from jax.sharding import PartitionSpec as P


def electron_term(phase, wann_real, wann_imag):
    real_part = jnp.einsum(
        "ke,peb->kpb", phase[0], wann_real, preferred_element_type=jnp.float32
    ) - jnp.einsum("ke,peb->kpb", phase[1], wann_imag, preferred_element_type=jnp.float32)
    imag_part = jnp.einsum(
        "ke,peb->kpb", phase[0], wann_imag, preferred_element_type=jnp.float32
    ) + jnp.einsum("ke,peb->kpb", phase[1], wann_real, preferred_element_type=jnp.float32)
    return jnp.stack([real_part, imag_part])


def body(g_wann, phonon_phase, electron_phase):
    local_vectors = g_wann.shape[2]
    offset = lax.axis_index("re") * local_vectors
    own_phase = lax.dynamic_slice_in_dim(electron_phase, offset, local_vectors, 2)
    partial_value = electron_term(own_phase, g_wann[0], g_wann[1])
    summed = lax.psum_scatter(partial_value, "re", scatter_dimension=1, tiled=True)
    bloch = summed.astype(jnp.bfloat16)
    cos_table = phonon_phase[0]
    sin_table = phonon_phase[1]
    piece = lax.all_gather(bloch, "pb", axis=2, tiled=True)
    acc_real = jnp.einsum(
        "qp,kpb->kqb", cos_table, piece[0], preferred_element_type=jnp.float32
    ) - jnp.einsum("qp,kpb->kqb", sin_table, piece[1], preferred_element_type=jnp.float32)
    acc_imag = jnp.einsum(
        "qp,kpb->kqb", cos_table, piece[1], preferred_element_type=jnp.float32
    ) + jnp.einsum("qp,kpb->kqb", sin_table, piece[0], preferred_element_type=jnp.float32)
    acc_real, acc_imag = (acc_real, acc_imag)
    return jnp.stack([acc_real, acc_imag], axis=1)


def solution(mesh):
    placed = (P(None, "pb", ("grp", "re"), "ka"), P(None, "pb", None), P())
    return jax.shard_map(
        body,
        mesh=mesh,
        in_specs=placed,
        out_specs=P(("grp", "re"), None, "pb", "ka"),
        check_vma=False,
    )
```

profile of v0, /device:TPU:0, one launch (start us, length us, event | category | flops | bytes accessed | tf_op | source)
XLA Modules:
  0.0 110.9 jit_solution(2155230755220057174)
XLA Ops:
  6.5 0.0 copy-start
  6.5 0.0 reduce-scatter.2.cloned.1.call-start
  6.5 0.7 copy-done
  7.2 0.0 copy-start.1
  7.2 2.2 %fusion = f32[8,256,128]{2,0,1:T(8,128)S(1)} fusion(bf16[2,256,32,128]{3,2,1,0:T(8,128)(2,1)} %param.3, bf16[2,8,64]{2,1,0:T(8,128)(2,1)S(1)} %copy-done, s32[]{:T(128)S(6)} %select_n.3), kind=kOutput, calls=%fused_computation.2 | convolution fusion | flops 16777216 | bytes 3147780 | tf_op jit(solution)/shard_map/ke,peb->kpb/dot_general | solution.py:11
  9.4 2.0 %fusion.2 = f32[8,256,128]{2,0,1:T(8,128)S(1)} fusion(bf16[2,256,32,128]{3,2,1,0:T(8,128)(2,1)} %param.3, bf16[2,8,64]{2,1,0:T(8,128)(2,1)S(1)} %copy-done, s32[]{:T(128)S(6)} %add.18, s32[]{:T(128)S(6)} %select_n.3), kind=kOutput, calls=%fused_computation.4 | convolution fusion | flops 16777216 | bytes 3147784 | tf_op jit(solution)/shard_map/ke,peb->kpb/dot_general | solution.py:10
  11.5 0.0 copy-done.1
  11.5 0.5 fusion.21
  11.9 0.5 fusion.15
  12.4 0.1 pad_maximum_fusion
  12.5 1.7 %copy.9 = f32[2,8,256,128]{3,2,0,1:T(8,128)} copy(f32[2,8,256,128]{3,1,2,0:T(8,128)S(1)} %pad_maximum_fusion) | data formatting | bytes 4194304 | tf_op jit(solution)/shard_map/stack | solution.py:14
  14.2 0.0 copy-start.2
  14.2 0.0 reduce-scatter.2.cloned.1.call-update
  14.3 0.0 all-gather.2.cloned.1.call-start
  14.3 34.7 %reduce-scatter.2.cloned.1.call-done = f32[2,4,256,128]{3,2,0,1:T(8,128)} async-done(((f32[2,8,256,128]{3,2,0,1:T(8,128)}), f32[2,4,256,128]{3,2,0,1:T(8,128)}) %reduce-scatter.2.cloned.1.call-update) | async-done | bytes 1048592 | tf_op jit(solution)/shard_map/reduce_scatter | solution.py:22
  49.0 2.2 %copy.10 = bf16[2,4,256,128]{2,3,1,0:T(8,128)(2,1)} copy(f32[2,4,256,128]{3,2,0,1:T(8,128)} %reduce-scatter.2.cloned.1.call-done) | data formatting | bytes 1572864 | tf_op jit(solution)/shard_map/reduce_scatter | solution.py:22
  51.3 0.0 all-gather.2.cloned.1.call-update
  51.3 46.4 %all-gather.2.cloned.1.call-done = bf16[2,4,1024,128]{2,3,1,0:T(8,128)(2,1)} async-done(((bf16[2,4,256,128]{2,3,1,0:T(8,128)(2,1)}), bf16[2,4,1024,128]{2,3,1,0:T(8,128)(2,1)}) %all-gather.2.cloned.1.call-update) | async-done | bytes 2097168 | tf_op jit(solution)/shard_map/all_gather | solution.py:26
  97.7 0.0 copy-done.2
  97.7 0.0 copy-start.3
  97.7 2.1 %fusion.28 = f32[4,128,512]{2,1,0:T(8,128)S(1)} fusion(bf16[2,4,1024,128]{2,3,1,0:T(8,128)(2,1)} %all-gather.2.cloned.1.call-done, bf16[2,512,1024]{2,1,0:T(8,128)(2,1)S(1)} %copy-done.2), kind=kOutput, calls=%fused_computation.26 | convolution fusion | flops 536870912 | bytes 3145728 | tf_op jit(solution)/shard_map/qp,kpb->kqb/dot_general | solution.py:30
  99.8 0.0 copy-done.3
  99.8 0.7 fusion.30
  100.6 0.7 fusion.24
  101.3 0.7 fusion.25
  102.1 0.2 pad_maximum_fusion.1
  102.3 1.8 %copy.11 = f32[4,2,512,128]{3,2,1,0:T(8,128)} copy(f32[4,2,512,128]{2,3,0,1:T(8,128)S(1)} %pad_maximum_fusion.1) | data formatting | bytes 4194304 | tf_op jit(solution)/shard_map/stack | solution.py:34
Async XLA Ops:
  6.5 0.7 copy-start
  6.5 42.5 %reduce-scatter.2.cloned.1.call-start = ((), (), s32[]{:S(2)}) async-start(), calls=%async_computation.1 | async-start | bytes 3145728 | tf_op jit(solution)/shard_map/reduce_scatter | solution.py:22
  7.2 4.2 %copy-start.1 = (bf16[2,256,32,128]{3,2,1,0:T(8,128)(2,1)S(1)}, bf16[2,256,32,128]{3,2,1,0:T(8,128)(2,1)}, u32[]{:S(2)}) copy-start(bf16[2,256,32,128]{3,2,1,0:T(8,128)(2,1)} %param.3) | copy-start | bytes 12582916
  14.2 83.5 %copy-start.2 = (bf16[2,512,1024]{2,1,0:T(8,128)(2,1)S(1)}, bf16[2,512,1024]{2,1,0:T(8,128)(2,1)}, u32[]{:S(2)}) copy-start(bf16[2,512,1024]{2,1,0:T(8,128)(2,1)} %param.4) | copy-start | bytes 6291460
  14.3 83.4 %all-gather.2.cloned.1.call-start = ((), (), s32[]{:S(2)}) async-start(), calls=%async_computation.2 | async-start | bytes 2621440 | tf_op jit(solution)/shard_map/all_gather | solution.py:26
  97.7 2.1 %copy-start.3 = (bf16[2,4,1024,128]{2,3,1,0:T(8,128)(2,1)S(1)}, bf16[2,4,1024,128]{2,3,1,0:T(8,128)(2,1)}, u32[]{:S(2)}) copy-start(bf16[2,4,1024,128]{2,3,1,0:T(8,128)(2,1)} %all-gather.2.cloned.1.call-done) | copy-start | bytes 6291460
Sparse Core Ops, SparseCore 0:
  14.4 34.6 reduce-scatter.1
  51.4 46.2 all-gather.1
where the time goes:
time: 111 us
  waiting for transfers between devices  81.2 us (73%)
  between operations  13.5 us (12%)
  matrix products  9.5 us (9%)
  local copies, waits for them, and re-layouts  6.43 us (6%)
    all_gather x1, waiting for transfers between devices, body(): piece = lax.all_gather(bloch, 'pb', axis=2, tiled=True)  46.4 us
    reduce_scatter x1, waiting for transfers between devices, body(): lax.psum_scatter(partial_value, 're', scatter_dimension=1, tiled=True)  34.7 us
    reduce_scatter x1, local copies, waits for them, and re-layouts, body(): lax.psum_scatter(partial_value, 're', scatter_dimension=1, tiled=True)  2.22 us
  transfers between devices with their start and end apart: 2, of which 2 were waited for; matrix products, arithmetic and copies ran while one was open for 0% of the time, Pallas kernels for 0%

commit v1 on v0

--- a/solution.py
+++ b/solution.py
@@ -23,7 +23,14 @@
     bloch = summed.astype(jnp.bfloat16)
     cos_table = phonon_phase[0]
     sin_table = phonon_phase[1]
-    piece = lax.all_gather(bloch, "pb", axis=2, tiled=True)
+    ways, here = (lax.axis_size("pb"), lax.axis_index("pb"))
+    piece, reach = (bloch, 1)
+    while reach < ways:
+        theirs = lax.ppermute(piece, "pb", [(d, d ^ reach) for d in range(ways)])
+        mine_first = jnp.concatenate([piece, theirs], axis=2)
+        theirs_first = jnp.concatenate([theirs, piece], axis=2)
+        piece = jnp.where(here & reach == 0, mine_first, theirs_first)
+        reach = 2 * reach
     acc_real = jnp.einsum(
         "qp,kpb->kqb", cos_table, piece[0], preferred_element_type=jnp.float32
     ) - jnp.einsum("qp,kpb->kqb", sin_table, piece[1], preferred_element_type=jnp.float32)

time: 111 us -> 124 us (1.12)
  waiting for transfers between devices: 81.2 us -> 91.7 us
  starting transfers between devices: 0.04 us -> 4.01 us
  matrix products: 9.5 us -> 8.11 us
    ppermute x0 -> x2, waiting for transfers between devices: none -> 56.9 us  [body(): theirs = lax.ppermute(piece, 'pb', [(d, d ^ reach) for d in range(ways)])]
    all_gather x1 -> x0, waiting for transfers between devices: 46.4 us -> none  [body(): piece = lax.all_gather(bloch, 'pb', axis=2, tiled=True)]
    ppermute x0 -> x2, starting transfers between devices: none -> 4.01 us  [body(): theirs = lax.ppermute(piece, 'pb', [(d, d ^ reach) for d in range(ways)])]
    dot_general x1, matrix products: 2.12 us -> 0.74 us  [body(): jnp.einsum('qp,kpb->kqb', cos_table, piece[1], preferred_element_type=jnp...]
  transfers between devices with their start and end apart: 2 -> 3, of which waited for: 2 -> 3; matrix products, arithmetic and copies ran while one was open for 0% -> 0% of each run, Pallas kernels for 0% -> 0%
where the time goes in v1:
time: 124 us
  waiting for transfers between devices  91.7 us (74%)
  between operations  13.5 us (11%)
  matrix products  8.11 us (7%)
  local copies, waits for them, and re-layouts  5.63 us (5%)
  starting transfers between devices  4.01 us (3%)
  other arithmetic  1.24 us (1%)
    ppermute x2, waiting for transfers between devices, body(): theirs = lax.ppermute(piece, 'pb', [(d, d ^ reach) for d in range(ways)])  56.9 us
    reduce_scatter x1, waiting for transfers between devices, body(): lax.psum_scatter(partial_value, 're', scatter_dimension=1, tiled=True)  34.8 us
    ppermute x2, starting transfers between devices, body(): theirs = lax.ppermute(piece, 'pb', [(d, d ^ reach) for d in range(ways)])  4.01 us
  transfers between devices with their start and end apart: 3, of which 3 were waited for; matrix products, arithmetic and copies ran while one was open for 0% of the time, Pallas kernels for 0%

profile of v1, /device:TPU:0, one launch (start us, length us, event | category | flops | bytes accessed | tf_op | source)
XLA Modules:
  0.0 124.1 jit_solution(8773569732101580187)
XLA Ops:
  6.5 0.0 copy-start
  6.5 0.0 reduce-scatter.2.cloned.1.call-start
  6.5 0.7 copy-done
  7.2 0.0 copy-start.1
  7.2 2.2 %fusion = f32[8,256,128]{2,0,1:T(8,128)S(1)} fusion(bf16[2,256,32,128]{3,2,1,0:T(8,128)(2,1)} %param.3, bf16[2,8,64]{2,1,0:T(8,128)(2,1)S(1)} %copy-done, s32[]{:T(128)S(6)} %select_n.21), kind=kOutput, calls=%fused_computation.3 | convolution fusion | flops 16777216 | bytes 3147780 | tf_op jit(solution)/shard_map/ke,peb->kpb/dot_general | solution.py:11
  9.4 2.0 %fusion.2 = f32[8,256,128]{2,0,1:T(8,128)S(1)} fusion(bf16[2,256,32,128]{3,2,1,0:T(8,128)(2,1)} %param.3, bf16[2,8,64]{2,1,0:T(8,128)(2,1)S(1)} %copy-done, s32[]{:T(128)S(6)} %add.18, s32[]{:T(128)S(6)} %select_n.21), kind=kOutput, calls=%fused_computation.5 | convolution fusion | flops 16777216 | bytes 3147784 | tf_op jit(solution)/shard_map/ke,peb->kpb/dot_general | solution.py:10
  11.5 0.0 copy-done.1
  11.5 0.5 fusion.15
  11.9 0.5 fusion.21
  12.4 0.1 pad_maximum_fusion
  12.5 1.7 %copy.9 = f32[2,8,256,128]{3,2,0,1:T(8,128)} copy(f32[2,8,256,128]{3,1,2,0:T(8,128)S(1)} %pad_maximum_fusion) | data formatting | bytes 4194304 | tf_op jit(solution)/shard_map/stack | solution.py:14
  14.2 0.0 reduce-scatter.2.cloned.1.call-update
  14.3 34.8 %reduce-scatter.2.cloned.1.call-done = f32[2,4,256,128]{3,2,0,1:T(8,128)} async-done(((f32[2,8,256,128]{3,2,0,1:T(8,128)}), f32[2,4,256,128]{3,2,0,1:T(8,128)}) %reduce-scatter.2.cloned.1.call-update) | async-done | bytes 1048592 | tf_op jit(solution)/shard_map/reduce_scatter | solution.py:22
  49.0 1.4 %copy.10 = bf16[2,4,256,128]{2,3,1,0:T(8,128)(2,1)S(1)} copy(f32[2,4,256,128]{3,2,0,1:T(8,128)} %reduce-scatter.2.cloned.1.call-done) | data formatting | bytes 1572864 | tf_op jit(solution)/shard_map/reduce_scatter | solution.py:22
  50.5 1.5 %collective-permute-start = (bf16[2,4,256,128]{2,3,1,0:T(8,128)(2,1)S(1)}, bf16[2,4,256,128]{2,3,1,0:T(8,128)(2,1)S(1)}, u32[]{:S(2)}, u32[]{:S(2)}) collective-permute-start(bf16[2,4,256,128]{2,3,1,0:T(8,128)(2,1)S(1)} %copy.10), channel_id=1, source_target_pairs={{0,4},{4,0},{8,12},{12,8},{1,5},{5,1},{9,13},{13,9},{2,6},{6,2},{1... | collective-permute-start | bytes 1572872 | tf_op jit(solution)/shard_map/ppermute | solution.py:29
  52.0 12.0 %collective-permute-done = bf16[2,4,256,128]{2,3,1,0:T(8,128)(2,1)S(1)} collective-permute-done((bf16[2,4,256,128]{2,3,1,0:T(8,128)(2,1)S(1)}, bf16[2,4,256,128]{2,3,1,0:T(8,128)(2,1)S(1)}, u32[]{:S(2)}, u32[]{:S(2)}) %collective-permute-start) | collective-permute-done | bytes 524320 | tf_op jit(solution)/shard_map/ppermute | solution.py:29
  64.0 0.3 maximum_select_fusion.1
  64.3 2.5 %collective-permute-start.1 = (bf16[2,4,512,128]{2,3,1,0:T(8,128)(2,1)S(1)}, bf16[2,4,512,128]{2,3,1,0:T(8,128)(2,1)S(1)}, u32[]{:S(2)}, u32[]{:S(2)}) collective-permute-start(bf16[2,4,512,128]{2,3,1,0:T(8,128)(2,1)S(1)} %maximum_select_fusion.1), channel_id=1, source_target_pairs={{0,8},{4,12},{8,0},{12,4},{1,9},{5,13},{9,1},{13,5},{2,10},{6,14},... | collective-permute-start | bytes 3145736 | tf_op jit(solution)/shard_map/ppermute | solution.py:29
  66.8 0.0 copy-start.2
  66.8 44.9 %collective-permute-done.1 = bf16[2,4,512,128]{2,3,1,0:T(8,128)(2,1)S(1)} collective-permute-done((bf16[2,4,512,128]{2,3,1,0:T(8,128)(2,1)S(1)}, bf16[2,4,512,128]{2,3,1,0:T(8,128)(2,1)S(1)}, u32[]{:S(2)}, u32[]{:S(2)}) %collective-permute-start.1) | collective-permute-done | bytes 1048608 | tf_op jit(solution)/shard_map/ppermute | solution.py:29
  111.6 0.7 maximum_select_fusion
  112.3 0.0 copy-done.2
  112.3 0.7 fusion.28
  113.1 0.7 fusion.26
  113.8 0.7 fusion.25
  114.6 0.7 fusion.24
  115.3 0.2 pad_maximum_fusion.1
  115.5 1.8 %copy.11 = f32[4,2,512,128]{3,2,1,0:T(8,128)} copy(f32[4,2,512,128]{2,3,0,1:T(8,128)S(1)} %pad_maximum_fusion.1) | data formatting | bytes 4194304 | tf_op jit(solution)/shard_map/stack | solution.py:41
Async XLA Ops:
  6.5 0.7 copy-start
  6.5 42.5 %reduce-scatter.2.cloned.1.call-start = ((), (), s32[]{:S(2)}) async-start(), calls=%async_computation.1 | async-start | bytes 3145728 | tf_op jit(solution)/shard_map/reduce_scatter | solution.py:22
  7.2 4.2 %copy-start.1 = (bf16[2,256,32,128]{3,2,1,0:T(8,128)(2,1)S(1)}, bf16[2,256,32,128]{3,2,1,0:T(8,128)(2,1)}, u32[]{:S(2)}) copy-start(bf16[2,256,32,128]{3,2,1,0:T(8,128)(2,1)} %param.3) | copy-start | bytes 12582916
  50.5 13.6 %collective-permute-start = (bf16[2,4,256,128]{2,3,1,0:T(8,128)(2,1)S(1)}, bf16[2,4,256,128]{2,3,1,0:T(8,128)(2,1)S(1)}, u32[]{:S(2)}, u32[]{:S(2)}) collective-permute-start(bf16[2,4,256,128]{2,3,1,0:T(8,128)(2,1)S(1)} %copy.10), channel_id=1, source_target_pairs={{0,4},{4,0},{8,12},{12,8},{1,5},{5,1},{9,13},{13,9},{2,6},{6,2},{1... | collective-permute-start | bytes 1572872 | tf_op jit(solution)/shard_map/ppermute | solution.py:29
  64.3 47.3 %collective-permute-start.1 = (bf16[2,4,512,128]{2,3,1,0:T(8,128)(2,1)S(1)}, bf16[2,4,512,128]{2,3,1,0:T(8,128)(2,1)S(1)}, u32[]{:S(2)}, u32[]{:S(2)}) collective-permute-start(bf16[2,4,512,128]{2,3,1,0:T(8,128)(2,1)S(1)} %maximum_select_fusion.1), channel_id=1, source_target_pairs={{0,8},{4,12},{8,0},{12,4},{1,9},{5,13},{9,1},{13,5},{2,10},{6,14},... | collective-permute-start | bytes 3145736 | tf_op jit(solution)/shard_map/ppermute | solution.py:29
  66.8 45.5 %copy-start.2 = (bf16[2,512,1024]{2,1,0:T(8,128)(2,1)S(1)}, bf16[2,512,1024]{2,1,0:T(8,128)(2,1)}, u32[]{:S(2)}) copy-start(bf16[2,512,1024]{2,1,0:T(8,128)(2,1)} %param.4) | copy-start | bytes 6291460
Sparse Core Ops, SparseCore 0:
  14.4 34.6 reduce-scatter.1
